TPU v7x, 512 devices: a whole 4x4x16 slice. The times are simulated.
512 devices in a mesh: tm: 16 (over z), expert: 32 (over x, y, core).
Axes of the slice: x: 4, y: 4, z: 16, core: 2. Of those that a mesh axis runs over, the one named last changes fastest.
Arguments:
- x_in: float32 [32, 4096, 1024], P('expert', 'tm'), may hold values from -6 to 6
- z_gate: bfloat16 [32, 4096, 1024], P('expert', 'tm'), may hold values from -6 to 6
- b_proj: float32 [32, 4096, 128], P('expert', 'tm'), may hold values from -1.5 to 1.5
- c_proj: float32 [32, 4096, 128], P('expert', 'tm'), may hold values from -1.5 to 1.5
- decay_log: float32 [32, 4096, 16], P('expert', 'tm'), as said below
- skip_gain: float32 [16], replicated, may hold values from 0.5 to 2
- residual: float32 [32, 4096, 1024], P('expert', 'tm'), may hold values from -6 to 6
- ssd_gain: float32 [1024], replicated, may hold values from 0.5 to 1.5
- moe_gain: float32 [1024], replicated, may hold values from 0.5 to 1.5
- w_gate: bfloat16 [32, 1024, 1536], P('expert', 'tm'), may hold values from -0.1875 to 0.1875
- w_up: bfloat16 [32, 1024, 1536], P('expert', 'tm'), may hold values from -0.1875 to 0.1875
- w_down: bfloat16 [32, 1536, 1024], P('expert', 'tm'), may hold values from -0.15625 to 0.15625
- routes: int32 [32, 4096, 2], P('expert', 'tm'), may hold values from 0 to 31, all different within a row; in each aligned block of 256 rows (0 to 255, 256 to 511, ..., all dimensions but the last counted through in order) at most 24 rows name the same one
- route_weights: float32 [32, 4096, 2], P('expert', 'tm'), may hold values from 0.2 to 1
Outputs:
- mixed: float32 [32, 4096, 1024], P('expert', 'tm')
Inputs may be any that keep to these rules, and one draw needn't show every extreme that they name: `routes`: the two experts of a time step differ. Among the time steps of one device no expert is named more than 24 times, and in every draw some device names some expert exactly 24 times. `decay_log`: every entry is at most zero.
All inputs are finite; a program needn't handle non-finite values.
Results may differ from a plain program's by a relative error of at most 0.0021.
Values may be sent and summed in bfloat16 or wider, within the bound.
No kernel may reach another device: no remote copies, remote signals or barrier semaphores. Data moves between devices by JAX's collectives and lax.ppermute only.
A program may use at most 64 MiB of HBM per device.

v0:
```python
import math
import jax
import jax.numpy as jnp
from jax import lax
from jax.sharding import PartitionSpec as P

exact_mode = lax.Precision.HIGHEST


def carried_in_2(value, axis, join, neutral):
    count, mine = (lax.axis_size(axis), lax.axis_index(axis))
    pieces = jax.tree.map(lambda part: lax.all_gather(part, axis), value)
    running = jax.tree.map(
        lambda part, zero: jnp.full_like(part, 0) + jnp.asarray(zero, part.dtype), value, neutral
    )

    def lap(position, running):
        longer = join(running, jax.tree.map(lambda part: part[position], pieces))
        return jax.tree.map(lambda new, old: jnp.where(position < mine, new, old), longer, running)

    return lax.fori_loop(0, count - 1, lap, running)


def group_carry(state, values, b_rows, running):
    remains = jnp.exp(running[-1][None, :] - running)
    fresh = jnp.einsum("jhp,jn->hpn", values * remains[:, :, None], b_rows, precision=exact_mode)
    return jnp.exp(running[-1])[:, None, None] * state + fresh


def group_step(state, inputs, skip_gain):
    values, b_rows, c_rows, log_rates = inputs
    length = values.shape[0]
    running = jnp.cumsum(log_rates, axis=0)
    across = running.T[:, :, None] - running.T[:, None, :]
    places = jnp.arange(length)
    causal = (places[:, None] >= places[None, :])[None]
    masked = jnp.where(causal, jnp.exp(jnp.where(causal, across, 0.0)), 0.0)
    scores = jnp.dot(c_rows, b_rows.T, precision=exact_mode)
    mixing = masked * scores[None]
    output = jnp.einsum("hij,jhp->ihp", mixing, values, precision=exact_mode)
    output = output + jnp.exp(running)[:, :, None] * jnp.einsum(
        "in,hpn->ihp", c_rows, state, precision=exact_mode
    )
    output = output + skip_gain[None, :, None] * values
    return (group_carry(state, values, b_rows, running), output)


def incoming_state(through, local_end):

    def combine(earlier, later):
        return (earlier[0] * later[0], later[0][:, None, None] * earlier[1] + later[1])

    prefix = carried_in_2(
        (through, local_end), "tm", combine, (jnp.ones_like(through), jnp.zeros_like(local_end))
    )
    return prefix[1]


def rms_scale(rows, gain):
    return gain * rows / jnp.sqrt(jnp.mean(rows * rows, axis=-1, keepdims=True) + 1e-05)


def per_device(
    x_in,
    z_gate,
    b_proj,
    c_proj,
    decay_log,
    skip_gain,
    residual,
    ssd_gain,
    moe_gain,
    w_gate,
    w_up,
    w_down,
    routes,
    route_weights,
):
    heads = skip_gain.shape[0]
    model_width = x_in.shape[2]
    width = model_width // heads
    length = x_in.shape[1]
    block = math.gcd(length, 256)
    count = length // block
    values = x_in[0].reshape(length, heads, width)
    b_rows = b_proj[0]
    c_rows = c_proj[0]
    log_rates = decay_log[0]
    inputs = (
        values.reshape(count, block, heads, width),
        b_rows.reshape(count, block, -1),
        c_rows.reshape(count, block, -1),
        log_rates.reshape(count, block, heads),
    )
    start = jnp.zeros((heads, width, b_rows.shape[1]), jnp.float32)
    through = jnp.exp(jnp.sum(log_rates, axis=0))
    local_end, outputs = lax.scan(
        lambda state, piece: group_step(state, piece, skip_gain), start, inputs
    )
    incoming = incoming_state(through, local_end)
    running = jnp.cumsum(log_rates, axis=0)
    carried_in = jnp.exp(running)[:, :, None] * jnp.einsum(
        "in,hpn->ihp", c_rows, incoming, precision=exact_mode
    )
    mixed_ssd = (outputs.reshape(length, heads, width) + carried_in).reshape(length, model_width)
    gated = mixed_ssd * jax.nn.silu(z_gate[0].astype(jnp.float32))
    hres = residual[0] + rms_scale(gated, ssd_gain)
    normed = rms_scale(hres, moe_gain).astype(jnp.bfloat16)
    expert_count = lax.axis_size("expert")
    capacity = max(2, 3 * length // expert_count)
    flat_routes = routes[0].reshape(-1)
    picked_one = (flat_routes[:, None] == jnp.arange(expert_count)[None, :]).astype(jnp.int32)
    earlier_hits = jnp.cumsum(picked_one, axis=0) - picked_one
    slot_index = jnp.sum(earlier_hits * picked_one, axis=1)
    target = flat_routes * capacity + slot_index
    repeated = jnp.broadcast_to(normed[:, None, :], (length, 2, model_width)).reshape(
        2 * length, model_width
    )
    outgoing = (
        jnp.zeros((expert_count * capacity, model_width), jnp.bfloat16).at[target].set(repeated)
    )
    received = lax.all_to_all(
        outgoing.reshape(expert_count, capacity, model_width),
        "expert",
        split_axis=0,
        concat_axis=0,
        tiled=True,
    )
    received = received.reshape(expert_count * capacity, model_width)
    slot_rows = expert_count * capacity
    columns = received
    gate = jnp.dot(
        columns,
        lax.all_gather(w_gate[0], "tm", axis=0, tiled=True),
        preferred_element_type=jnp.float32,
    )
    upper = jnp.dot(
        columns,
        lax.all_gather(w_up[0], "tm", axis=0, tiled=True),
        preferred_element_type=jnp.float32,
    )
    hidden = (jax.nn.silu(gate) * upper).astype(jnp.bfloat16)
    columns = hidden
    produced = jnp.dot(
        columns,
        lax.all_gather(w_down[0], "tm", axis=0, tiled=True),
        preferred_element_type=jnp.float32,
    ).astype(jnp.bfloat16)
    back = lax.all_to_all(
        produced.reshape(expert_count, capacity, model_width),
        "expert",
        split_axis=0,
        concat_axis=0,
        tiled=True,
    )
    back = back.reshape(slot_rows, model_width)
    fetched = back[target].astype(jnp.float32).reshape(length, 2, model_width)
    weights_here = route_weights[0]
    moe = fetched[:, 0, :] * weights_here[:, 0:1] + fetched[:, 1, :] * weights_here[:, 1:2]
    return (hres + moe).reshape(1, length, model_width)


def solution(mesh):
    in_specs = (
        P("expert", "tm", None),
        P("expert", "tm", None),
        P("expert", "tm", None),
        P("expert", "tm", None),
        P("expert", "tm", None),
        P(),
        P("expert", "tm", None),
        P(),
        P(),
        P("expert", "tm", None),
        P("expert", "tm", None),
        P("expert", "tm", None),
        P("expert", "tm", None),
        P("expert", "tm", None),
    )
    out_specs = P("expert", "tm", None)
    return jax.shard_map(
        per_device, mesh=mesh, in_specs=in_specs, out_specs=out_specs, check_vma=False
    )
```

profile of v0, /device:TPU:1, one launch (start us, length us, event | category | flops | bytes accessed | tf_op | source)
XLA Modules:
  0.0 405.9 jit_solution(9429766804105325587)
XLA Ops:
  6.5 0.8 copy_bitcast_fusion.3
  7.3 0.6 reduce-window.16
  8.5 1.6 copy.54
  10.2 1.8 convolution_add_fusion
  12.0 0.7 all-gather.12.cloned.1.call-update
  12.8 0.7 all-gather.14.cloned.1.call-update
  15.0 1.3 dynamic-slice
  17.1 32.2 %all-reduce = f32[256]{0:T(256)S(1)} all-reduce(f32[256]{0:T(256)S(1)} %exponential_dynamic-update-slice_fusion), channel_id=2, replica_groups=mesh['tm'=16,'expert'=32] {'tm'}, use_global_device_ids=true, to_apply=%add | all-reduce | flops 256 | bytes 2048
  49.4 1.2 copy.57
  50.6 1.2 reduce-window.24
  52.4 5.1 %fusion.24 = f32[256,16,64]{0,2,1:T(8,128)S(1)} fusion(f32[256,16,64]{0,2,1:T(8,128)S(1)} %bitcast.161, f32[256,256]{1,0:T(8,128)S(1)} %fusion.49, f32[16,256]{1,0:T(8,128)S(1)} %get-tuple-element.159, pred[256,256]{1,0:T(8,128)(4,1)S(1)} %iota_compare_fusion), kind=kOutput, calls=%fused_computation.23 | convolution fusion | flops 809500672 | bytes 2441216 | tf_op jit(solution)/shard_map/while/body/eval_jaxpr/hij,jhp->ihp/dot_general | solution.py:40
  57.6 2.1 fusion.31
  59.7 64.1 %all-gather.10.cloned.1.call-done = f32[256,64,128]{2,1,0:T(8,128)} async-done(((f32[16,64,128]{2,1,0:T(8,128)}), f32[256,64,128]{2,1,0:T(8,128)}) %all-gather.10.cloned.1.call-update) | async-done | bytes 8388624 | tf_op jit(solution)/shard_map/all_gather | solution.py:12
  123.7 18.2 %while.9 = (s32[]{:T(128)}, f32[16,64,128]{2,1,0:T(8,128)S(1)}, s32[]{:T(128)}, f32[16,16]{1,0:T(8,128)S(1)}, f32[16,16,64,128]{3,2,1,0:T(8,128)}, /*index=5*/s32[]{:T(128)}, s32[]{:T(128)}) while((s32[]{:T(128)}, f32[16,64,128]{2,1,0:T(8,128)S(1)}, s32[]{:T(128)}, f32[16,16]{1,0:T(8,128)S(1)}, f32[16,16,64,128]{3,2,1,0:T(8,128)}, ...), condition=%wide.region_4.5_spmd.clone, body=%wide.region_3.4_spmd.clone.sunk | while | flops 524292 | bytes 1573161 | solution.py:21
  123.8 1.2 fusion.70
  125.0 1.2 fusion.70
  126.2 1.2 fusion.70
  127.4 1.2 fusion.70
  128.6 1.2 fusion.70
  129.8 1.2 fusion.70
  131.0 1.2 fusion.70
  132.2 1.2 fusion.70
  133.5 1.2 fusion.70
  134.7 1.2 fusion.70
  135.9 1.2 fusion.70
  137.1 1.2 fusion.70
  138.3 1.2 fusion.70
  139.5 1.2 fusion.70
  140.8 1.2 fusion.70
  142.0 2.8 multiply_reduce_fusion.1
  144.8 1.3 copy.62
  146.1 1.8 multiply_reduce_fusion
  148.1 0.5 broadcast_in_dim.66
  148.7 1.2 reshape.351
  149.9 4.5 %scatter_custom_fusion = bf16[768,1024]{1,0:T(8,128)(2,1)} fusion(s32[512]{0:T(512)S(1)} %bitcast.171, bf16[512,1024]{1,0:T(8,128)(2,1)} %reshape.351, bf16[]{:T(256)} %constant.72.clone.1), kind=kCustom, calls=%fused_computation.51 | custom fusion | bytes 1573376 | tf_op jit(solution)/shard_map/scatter | solution.py:120
  154.4 7.5 %all-to-all-start = ((bf16[32,24,1024]{2,1,0:T(8,128)(2,1)}), bf16[32,24,1024]{2,1,0:T(8,128)(2,1)S(1)}, u32[]{:S(2)}, u32[]{:S(2)}) async-start(bf16[32,24,1024]{2,1,0:T(8,128)(2,1)} %bitcast.23), calls=%async_computation | async-start | bytes 3145728 | tf_op jit(solution)/shard_map/all_to_all | solution.py:122
  162.0 29.4 %all-gather.12.cloned.1.call-done = bf16[1,1024,1536]{2,1,0:T(8,128)(2,1)} async-done(((bf16[1,64,1536]{2,1,0:T(8,128)(2,1)}), bf16[1,1024,1536]{2,1,0:T(8,128)(2,1)}) %all-gather.12.cloned.1.call-update) | async-done | bytes 3145744 | tf_op jit(solution)/shard_map/all_gather | solution.py:134
  191.3 6.1 %fusion.10 = f32[768,1536]{1,0:T(8,128)} fusion(bf16[768,1024]{1,0:T(8,128)(2,1)S(1)} %bitcast.166, bf16[1,1024,1536]{2,1,0:T(8,128)(2,1)} %all-gather.12.cloned.1.call-done), kind=kOutput, calls=%fused_computation.15 | convolution fusion | flops 2415919104 | bytes 9437184 | tf_op jit(solution)/shard_map/dot_general | solution.py:132
  197.4 69.0 %all-gather.14.cloned.1.call-done = bf16[1,1024,1536]{2,1,0:T(8,128)(2,1)} async-done(((bf16[1,64,1536]{2,1,0:T(8,128)(2,1)}), bf16[1,1024,1536]{2,1,0:T(8,128)(2,1)}) %all-gather.14.cloned.1.call-update) | async-done | bytes 3145744 | tf_op jit(solution)/shard_map/all_gather | solution.py:139
  266.4 75.2 %all-gather.16.cloned.1.call-done = bf16[1,1536,1024]{2,1,0:T(8,128)(2,1)} async-done(((bf16[1,96,1024]{2,1,0:T(8,128)(2,1)}), bf16[1,1536,1024]{2,1,0:T(8,128)(2,1)}) %all-gather.16.cloned.1.call-update) | async-done | bytes 3145744 | tf_op jit(solution)/shard_map/all_gather | solution.py:146
  341.6 10.5 %fusion.19 = bf16[768,1024]{1,0:T(8,128)(2,1)} fusion(bf16[1,1536,1024]{2,1,0:T(8,128)(2,1)} %all-gather.16.cloned.1.call-done, f32[768,1536]{1,0:T(8,128)} %fusion.10, bf16[768,1024]{1,0:T(8,128)(2,1)S(1)} %bitcast.167, bf16[1,1024,1536]{2,1,0:T(8,128)(2,1)} %all-gather.14.cloned.1.call-done), kind=kOutput, calls=%fused_computation.22 | convolution fusion | flops 4839702528 | bytes 14155776 | tf_op jit(solution)/shard_map/dot_general | solution.py:144
  352.0 16.2 %all-to-all-start.1 = ((bf16[32,24,1024]{2,1,0:T(8,128)(2,1)}), bf16[32,24,1024]{2,1,0:T(8,128)(2,1)S(1)}, u32[]{:S(2)}, u32[]{:S(2)}) async-start(bf16[32,24,1024]{2,1,0:T(8,128)(2,1)} %bitcast.168), calls=%async_computation.1 | async-start | bytes 3145728 | tf_op jit(solution)/shard_map/all_to_all | solution.py:149
  368.3 1.3 copy.56
  369.6 21.3 %all-to-all-done.1 = bf16[32,24,1024]{2,1,0:T(8,128)(2,1)S(1)} async-done(((bf16[32,24,1024]{2,1,0:T(8,128)(2,1)}), bf16[32,24,1024]{2,1,0:T(8,128)(2,1)S(1)}, u32[]{:S(2)}, u32[]{:S(2)}) %all-to-all-start.1) | async-done | bytes 1572896 | tf_op jit(solution)/shard_map/all_to_all | solution.py:149
  390.9 2.8 gather_fusion
  393.7 2.4 reshape.338
  396.1 1.6 fusion.61
  397.7 1.6 fusion.34
  (78 shorter events, 3.5 us)
Async XLA Ops:
  6.5 8.1 %copy-start = (f32[1,256,128]{2,1,0:T(8,128)S(1)}, f32[1,256,128]{2,1,0:T(8,128)}, u32[]{:S(2)}) copy-start(f32[1,256,128]{2,1,0:T(8,128)} %param.19) | copy-start | bytes 393220
  6.5 3.6 copy-start.5
  6.5 117.2 %all-gather.10.cloned.1.call-start = ((), (), s32[]{:S(2)}) async-start(), calls=%async_computation.2 | async-start | bytes 8912896 | tf_op jit(solution)/shard_map/all_gather | solution.py:12
  8.4 5.6 %copy-start.6 = (f32[1,256,16]{1,2,0:T(8,128)S(1)}, f32[1,256,16]{1,2,0:T(8,128)}, u32[]{:S(2)}) copy-start(f32[1,256,16]{1,2,0:T(8,128)} %param.20) | copy-start | bytes 49156
  8.5 5.7 %copy-start.8 = (s32[1,256,2]{1,2,0:T(2,128)S(1)}, s32[1,256,2]{1,2,0:T(2,128)}, u32[]{:S(2)}) copy-start(s32[1,256,2]{1,2,0:T(2,128)} %param.28) | copy-start | bytes 6148
  10.0 39.4 %copy-start.1 = (bf16[1,256,1024]{2,1,0:T(8,128)(2,1)S(1)}, bf16[1,256,1024]{2,1,0:T(8,128)(2,1)}, u32[]{:S(2)}) copy-start(bf16[1,256,1024]{2,1,0:T(8,128)(2,1)} %param.17) | copy-start | bytes 1572868
  12.0 179.4 %all-gather.12.cloned.1.call-start = ((), (), s32[]{:S(2)}) async-start(), calls=%async_computation.3 | async-start | bytes 3342336 | tf_op jit(solution)/shard_map/all_gather | solution.py:134
  12.7 253.7 %all-gather.14.cloned.1.call-start = ((), (), s32[]{:S(2)}) async-start(), calls=%async_computation.4 | async-start | bytes 3342336 | tf_op jit(solution)/shard_map/all_gather | solution.py:139
  13.4 328.1 %all-gather.16.cloned.1.call-start = ((), (), s32[]{:S(2)}) async-start(), calls=%async_computation.5 | async-start | bytes 3342336 | tf_op jit(solution)/shard_map/all_gather | solution.py:146
  52.4 5.1 %copy-start.11 = (f32[16]{0:T(128)S(1)}, f32[16]{0:T(128)}, u32[]{:S(2)}) copy-start(f32[16]{0:T(128)} %param.21) | copy-start | bytes 196
  142.0 4.2 %copy-start.3 = (f32[1,256,1024]{2,1,0:T(8,128)S(1)}, f32[1,256,1024]{2,1,0:T(8,128)}, u32[]{:S(2)}) copy-start(f32[1,256,1024]{2,1,0:T(8,128)} %param.22) | copy-start | bytes 3145732
  142.0 4.1 %copy-start.7 = (f32[1024]{0:T(1024)S(1)}, f32[1024]{0:T(1024)}, u32[]{:S(2)}) copy-start(f32[1024]{0:T(1024)} %param.23) | copy-start | bytes 12292
  144.8 3.1 copy-start.9
  154.4 36.9 %all-to-all-start = ((bf16[32,24,1024]{2,1,0:T(8,128)(2,1)}), bf16[32,24,1024]{2,1,0:T(8,128)(2,1)S(1)}, u32[]{:S(2)}, u32[]{:S(2)}) async-start(bf16[32,24,1024]{2,1,0:T(8,128)(2,1)} %bitcast.23), calls=%async_computation | async-start | bytes 3145728 | tf_op jit(solution)/shard_map/all_to_all | solution.py:122
  352.0 16.2 %copy-start.10 = (f32[1,256,2]{1,2,0:T(2,128)S(1)}, f32[1,256,2]{1,2,0:T(2,128)}, u32[]{:S(2)}) copy-start(f32[1,256,2]{1,2,0:T(2,128)} %param.29) | copy-start | bytes 6148
  352.0 38.9 %all-to-all-start.1 = ((bf16[32,24,1024]{2,1,0:T(8,128)(2,1)}), bf16[32,24,1024]{2,1,0:T(8,128)(2,1)S(1)}, u32[]{:S(2)}, u32[]{:S(2)}) async-start(bf16[32,24,1024]{2,1,0:T(8,128)(2,1)} %bitcast.168), calls=%async_computation.1 | async-start | bytes 3145728 | tf_op jit(solution)/shard_map/all_to_all | solution.py:149
  396.1 1.7 copy-start.2
  396.1 1.7 copy-start.4
Sparse Core Ops, SparseCore 0:
  12.1 111.6 all-gather.9
  125.8 65.4 all-gather.11
  193.4 72.9 all-gather.13
  268.3 73.2 all-gather.15
where the time goes:
time: 407 us; the launch traced here: 406 us
  waiting for transfers between devices  261 us (64%)
  blocking collectives  32.2 us (8%)
  matrix products  28.7 us (7%)
  starting transfers between devices  23.9 us (6%)
  other arithmetic  23.6 us (6%)
  local copies, waits for them, and re-layouts  22.1 us (5%)
  between operations  14.1 us (3%)
    all_gather x1, waiting for transfers between devices, per_device(): lax.all_gather(w_down[0], 'tm', axis=0, tiled=True)  75.2 us
    all_gather x1, waiting for transfers between devices, per_device(): lax.all_gather(w_up[0], 'tm', axis=0, tiled=True)  69 us
    all_gather x1, waiting for transfers between devices, carried_in_2(): pieces = jax.tree.map(lambda part: lax.all_gather(part, axis), value)  64.1 us
    unnamed x1, blocking collectives  32.2 us
    all_gather x1, waiting for transfers between devices, per_device(): lax.all_gather(w_gate[0], 'tm', axis=0, tiled=True)  29.4 us
    all_to_all x1, waiting for transfers between devices, per_device(): lax.all_to_all(produced.reshape(expert_count, capacity, model_width), 'ex...  21.3 us
    select_n x15, other arithmetic, lap(): jnp.where(position < mine, new, old)  17.6 us
    all_to_all x1, starting transfers between devices, per_device(): lax.all_to_all(produced.reshape(expert_count, capacity, model_width), 'ex...  16.2 us
  transfers between devices with their start and end apart: 6, of which 5 were waited for; matrix products, arithmetic and copies ran while one was open for 12% of the time, Pallas kernels for 0%

commit v1 on v0

--- a/solution.py
+++ b/solution.py
@@ -129,11 +129,11 @@
     received = received.reshape(expert_count * capacity, model_width)
     slot_rows = expert_count * capacity
     columns = received
-    gate = jnp.dot(
-        columns,
-        lax.all_gather(w_gate[0], "tm", axis=0, tiled=True),
-        preferred_element_type=jnp.float32,
+    indices_shape = lambda unit, named_axis: jnp.concatenate(
+        lax.all_to_all(jnp.stack(lax.axis_size(named_axis) * [unit], axis=0), named_axis, 0, 0),
+        axis=0,
     )
+    gate = jnp.dot(columns, indices_shape(w_gate[0], "tm"), preferred_element_type=jnp.float32)
     upper = jnp.dot(
         columns,
         lax.all_gather(w_up[0], "tm", axis=0, tiled=True),

time: 407 us -> 465 us (1.14)
  blocking collectives: 32.2 us -> 217 us
  waiting for transfers between devices: 261 us -> 123 us
  starting transfers between devices: 23.9 us -> 32.2 us
    unnamed x1, blocking collectives: 32.2 us -> 186 us
    all_gather x1, waiting for transfers between devices: 69 us -> 0.71 us  [per_device(): lax.all_gather(w_up[0], 'tm', axis=0, tiled=True)]
    all_gather x1, waiting for transfers between devices: 64.1 us -> 24.2 us  [carried_in_2(): pieces = jax.tree.map(lambda part: lax.all_gather(part, axis), value)]
    all_to_all x0 -> x1, blocking collectives: none -> 30.2 us  [per_device(): lax.all_to_all(outgoing.reshape(expert_count, capacity, model_width), 'ex...]
    all_gather x1 -> x0, waiting for transfers between devices: 29.4 us -> none  [per_device(): lax.all_gather(w_gate[0], 'tm', axis=0, tiled=True)]
    all_to_all x1, starting transfers between devices: 7.54 us -> 15.9 us  [per_device(): lax.all_to_all(jnp.stack(lax.axis_size(named_axis) * [unit], axis=0), nam...]
  transfers between devices with their start and end apart: 6 -> 5, of which waited for: 5 -> 4; matrix products, arithmetic and copies ran while one was open for 12% -> 11% of each run, Pallas kernels for 0% -> 0%
where the time goes in v1:
time: 465 us; the launch traced here: 463 us
  blocking collectives  217 us (47%)
  waiting for transfers between devices  123 us (26%)
  starting transfers between devices  32.2 us (7%)
  matrix products  29.1 us (6%)
  local copies, waits for them, and re-layouts  24.6 us (5%)
  other arithmetic  23.5 us (5%)
  between operations  14.1 us (3%)
    unnamed x1, blocking collectives  186 us
    all_gather x1, waiting for transfers between devices, per_device(): lax.all_gather(w_down[0], 'tm', axis=0, tiled=True)  75.1 us
    all_to_all x1, blocking collectives, per_device(): lax.all_to_all(outgoing.reshape(expert_count, capacity, model_width), 'ex...  30.2 us
    all_gather x1, waiting for transfers between devices, carried_in_2(): pieces = jax.tree.map(lambda part: lax.all_gather(part, axis), value)  24.2 us
    all_to_all x1, waiting for transfers between devices, per_device(): lax.all_to_all(produced.reshape(expert_count, capacity, model_width), 'ex...  21.3 us
    select_n x15, other arithmetic, lap(): jnp.where(position < mine, new, old)  17.6 us
    all_to_all x1, starting transfers between devices, per_device(): lax.all_to_all(produced.reshape(expert_count, capacity, model_width), 'ex...  16.2 us
    all_to_all x1, starting transfers between devices, per_device(): lax.all_to_all(jnp.stack(lax.axis_size(named_axis) * [unit], axis=0), nam...  15.9 us
  transfers between devices with their start and end apart: 5, of which 4 were waited for; matrix products, arithmetic and copies ran while one was open for 11% of the time, Pallas kernels for 0%

profile of v1, /device:TPU:1, one launch (start us, length us, event | category | flops | bytes accessed | tf_op | source)
XLA Modules:
  0.0 463.4 jit_solution(15332401351944107014)
XLA Ops:
  6.5 0.8 copy_bitcast_fusion.3
  8.5 1.6 copy.54
  10.2 1.8 convolution_add_fusion
  12.0 0.7 all-gather.10.cloned.1.call-update
  12.7 1.9 stack.3
  14.7 15.9 %all-to-all-start.1 = ((bf16[16,64,1536]{2,1,0:T(8,128)(2,1)}), bf16[16,64,1536]{2,1,0:T(8,128)(2,1)}, u32[]{:S(2)}, u32[]{:S(2)}) async-start(bf16[16,64,1536]{2,1,0:T(8,128)(2,1)} %stack.3), calls=%async_computation.1 | async-start | bytes 6291456 | tf_op jit(solution)/shard_map/all_to_all | solution.py:133
  30.6 0.7 all-gather.12.cloned.1.call-update
  31.9 1.3 dynamic-slice
  34.0 186.5 %all-reduce = f32[256]{0:T(256)S(1)} all-reduce(f32[256]{0:T(256)S(1)} %exponential_dynamic-update-slice_fusion), channel_id=2, replica_groups=mesh['tm'=16,'expert'=32] {'tm'}, use_global_device_ids=true, to_apply=%add | all-reduce | flops 256 | bytes 2048
  220.5 1.2 copy.57
  221.7 1.2 reduce-window.24
  224.0 5.1 %fusion.22 = f32[256,16,64]{0,2,1:T(8,128)S(1)} fusion(f32[256,16,64]{0,2,1:T(8,128)S(1)} %bitcast.161, f32[256,256]{1,0:T(8,128)S(1)} %fusion.47, f32[16,256]{1,0:T(8,128)S(1)} %get-tuple-element.159, pred[256,256]{1,0:T(8,128)(4,1)S(1)} %iota_compare_fusion), kind=kOutput, calls=%fused_computation.21 | convolution fusion | flops 809500672 | bytes 2441216 | tf_op jit(solution)/shard_map/while/body/eval_jaxpr/hij,jhp->ihp/dot_general | solution.py:40
  229.1 2.0 fusion.29
  231.2 24.2 %all-gather.8.cloned.1.call-done = f32[256,64,128]{2,1,0:T(8,128)} async-done(((f32[16,64,128]{2,1,0:T(8,128)}), f32[256,64,128]{2,1,0:T(8,128)}) %all-gather.8.cloned.1.call-update) | async-done | bytes 8388624 | tf_op jit(solution)/shard_map/all_gather | solution.py:12
  255.4 18.2 %while.9 = (s32[]{:T(128)}, f32[16,64,128]{2,1,0:T(8,128)S(1)}, s32[]{:T(128)}, f32[16,16]{1,0:T(8,128)S(1)}, f32[16,16,64,128]{3,2,1,0:T(8,128)}, /*index=5*/s32[]{:T(128)}, s32[]{:T(128)}) while((s32[]{:T(128)}, f32[16,64,128]{2,1,0:T(8,128)S(1)}, s32[]{:T(128)}, f32[16,16]{1,0:T(8,128)S(1)}, f32[16,16,64,128]{3,2,1,0:T(8,128)}, ...), condition=%wide.region_4.5_spmd.clone, body=%wide.region_3.4_spmd.clone.sunk | while | flops 524292 | bytes 1573161 | solution.py:21
  255.4 1.2 fusion.70
  256.6 1.2 fusion.70
  257.8 1.2 fusion.70
  259.0 1.2 fusion.70
  260.2 1.2 fusion.70
  261.4 1.2 fusion.70
  262.6 1.2 fusion.70
  263.9 1.2 fusion.70
  265.1 1.2 fusion.70
  266.3 1.2 fusion.70
  267.5 1.2 fusion.70
  268.7 1.2 fusion.70
  269.9 1.2 fusion.70
  271.1 1.2 fusion.70
  272.4 1.2 fusion.70
  273.6 2.8 multiply_reduce_fusion.1
  276.4 1.3 copy.62
  277.7 1.8 multiply_reduce_fusion
  280.2 1.2 reshape.356
  281.4 3.9 scatter_custom_fusion
  285.4 30.2 %all_to_all.15 = bf16[32,24,1024]{2,1,0:T(8,128)(2,1)S(1)} all-to-all(bf16[32,24,1024]{2,1,0:T(8,128)(2,1)S(1)} %bitcast.163), channel_id=1, replica_groups=mesh['tm'=16,'expert'=32] {'expert'}, dimensions={0} | all-to-all | bytes 3145728 | tf_op jit(solution)/shard_map/all_to_all | solution.py:122
  315.6 1.2 copy-done.5
  316.7 6.1 %fusion.61 = f32[768,1536]{1,0:T(8,128)} fusion(bf16[768,1024]{1,0:T(8,128)(2,1)S(1)} %bitcast.168, bf16[1024,1536]{1,0:T(8,128)(2,1)} %bitcast.26), kind=kOutput, calls=%fused_computation.88 | convolution fusion | flops 2415919104 | bytes 9437184 | tf_op jit(solution)/shard_map/dot_general | solution.py:136
  322.8 0.7 all-gather.10.cloned.1.call-done
  323.5 75.1 %all-gather.12.cloned.1.call-done = bf16[1,1536,1024]{2,1,0:T(8,128)(2,1)} async-done(((bf16[1,96,1024]{2,1,0:T(8,128)(2,1)}), bf16[1,1536,1024]{2,1,0:T(8,128)(2,1)}) %all-gather.12.cloned.1.call-update) | async-done | bytes 3145744 | tf_op jit(solution)/shard_map/all_gather | solution.py:146
  398.6 10.9 %fusion.17 = bf16[768,1024]{1,0:T(8,128)(2,1)} fusion(bf16[1,1536,1024]{2,1,0:T(8,128)(2,1)} %all-gather.12.cloned.1.call-done, f32[768,1536]{1,0:T(8,128)} %fusion.61, bf16[768,1024]{1,0:T(8,128)(2,1)} %bitcast.169, bf16[1,1024,1536]{2,1,0:T(8,128)(2,1)} %all-gather.10.cloned.1.call-done), kind=kOutput, calls=%fused_computation.20 | convolution fusion | flops 4839702528 | bytes 14155776 | tf_op jit(solution)/shard_map/dot_general | solution.py:144
  409.5 16.2 %all-to-all-start.2 = ((bf16[32,24,1024]{2,1,0:T(8,128)(2,1)}), bf16[32,24,1024]{2,1,0:T(8,128)(2,1)S(1)}, u32[]{:S(2)}, u32[]{:S(2)}) async-start(bf16[32,24,1024]{2,1,0:T(8,128)(2,1)} %bitcast.167), calls=%async_computation.2 | async-start | bytes 3145728 | tf_op jit(solution)/shard_map/all_to_all | solution.py:149
  425.7 1.3 copy.56
  427.1 21.3 %all-to-all-done.2 = bf16[32,24,1024]{2,1,0:T(8,128)(2,1)S(1)} async-done(((bf16[32,24,1024]{2,1,0:T(8,128)(2,1)}), bf16[32,24,1024]{2,1,0:T(8,128)(2,1)S(1)}, u32[]{:S(2)}, u32[]{:S(2)}) %all-to-all-start.2) | async-done | bytes 1572896 | tf_op jit(solution)/shard_map/all_to_all | solution.py:149
  448.4 2.8 gather_fusion
  451.2 2.4 reshape.343
  453.6 1.6 fusion.59
  455.2 1.6 fusion.32
  (81 shorter events, 4.1 us)
Async XLA Ops:
  6.5 217.1 %copy-start = (f32[1,256,128]{2,1,0:T(8,128)S(1)}, f32[1,256,128]{2,1,0:T(8,128)}, u32[]{:S(2)}) copy-start(f32[1,256,128]{2,1,0:T(8,128)} %param.19) | copy-start | bytes 393220
  6.5 3.6 copy-start.6
  6.5 248.8 %all-gather.8.cloned.1.call-start = ((), (), s32[]{:S(2)}) async-start(), calls=%async_computation.3 | async-start | bytes 8912896 | tf_op jit(solution)/shard_map/all_gather | solution.py:12
  8.4 4.3 copy-start.7
  12.0 311.5 %all-gather.10.cloned.1.call-start = ((), (), s32[]{:S(2)}) async-start(), calls=%async_computation.4 | async-start | bytes 3342336 | tf_op jit(solution)/shard_map/all_gather | solution.py:139
  14.7 16.7 %copy-start.8 = (f32[1,256,16]{1,2,0:T(8,128)S(1)}, f32[1,256,16]{1,2,0:T(8,128)}, u32[]{:S(2)}) copy-start(f32[1,256,16]{1,2,0:T(8,128)} %param.20) | copy-start | bytes 49156
  14.7 16.8 %copy-start.10 = (s32[1,256,2]{1,2,0:T(2,128)S(1)}, s32[1,256,2]{1,2,0:T(2,128)}, u32[]{:S(2)}) copy-start(s32[1,256,2]{1,2,0:T(2,128)} %param.28) | copy-start | bytes 6148
  14.7 205.9 %copy-start.1 = (bf16[1,256,1024]{2,1,0:T(8,128)(2,1)S(1)}, bf16[1,256,1024]{2,1,0:T(8,128)(2,1)}, u32[]{:S(2)}) copy-start(bf16[1,256,1024]{2,1,0:T(8,128)(2,1)} %param.17) | copy-start | bytes 1572868
  14.7 270.7 %all-to-all-start.1 = ((bf16[16,64,1536]{2,1,0:T(8,128)(2,1)}), bf16[16,64,1536]{2,1,0:T(8,128)(2,1)}, u32[]{:S(2)}, u32[]{:S(2)}) async-start(bf16[16,64,1536]{2,1,0:T(8,128)(2,1)} %stack.3), calls=%async_computation.1 | async-start | bytes 6291456 | tf_op jit(solution)/shard_map/all_to_all | solution.py:133
  30.6 368.0 %all-gather.12.cloned.1.call-start = ((), (), s32[]{:S(2)}) async-start(), calls=%async_computation.5 | async-start | bytes 3342336 | tf_op jit(solution)/shard_map/all_gather | solution.py:146
  224.0 5.1 %copy-start.13 = (f32[16]{0:T(128)S(1)}, f32[16]{0:T(128)}, u32[]{:S(2)}) copy-start(f32[16]{0:T(128)} %param.21) | copy-start | bytes 196
  273.5 4.2 copy-start.3
  273.6 4.1 copy-start.9
  276.4 3.1 copy-start.11
  315.6 1.2 copy-start.5
  409.5 16.2 %copy-start.12 = (f32[1,256,2]{1,2,0:T(2,128)S(1)}, f32[1,256,2]{1,2,0:T(2,128)}, u32[]{:S(2)}) copy-start(f32[1,256,2]{1,2,0:T(2,128)} %param.29) | copy-start | bytes 6148
  409.5 38.9 %all-to-all-start.2 = ((bf16[32,24,1024]{2,1,0:T(8,128)(2,1)}), bf16[32,24,1024]{2,1,0:T(8,128)(2,1)S(1)}, u32[]{:S(2)}, u32[]{:S(2)}) async-start(bf16[32,24,1024]{2,1,0:T(8,128)(2,1)} %bitcast.167), calls=%async_computation.2 | async-start | bytes 3145728 | tf_op jit(solution)/shard_map/all_to_all | solution.py:149
  453.5 1.7 copy-start.2
  453.5 1.7 copy-start.4
Sparse Core Ops, SparseCore 0:
  12.1 243.2 all-gather.7
  257.4 66.0 all-gather.9
  325.6 72.9 all-gather.11
